TPU v7x, 32 devices: a whole 2x2x4 slice. The times are simulated.
32 devices in a mesh: shard: 4 (over z), ctx: 4 (over x, core), tp: 2 (over y).
Axes of the slice: x: 2, y: 2, z: 4, core: 2. Of those that a mesh axis runs over, the one named last changes fastest.
Arguments:
- hidden_in: bfloat16 [4, 1024, 1024], P('shard', 'ctx'), may hold values from -6 to 6
- out_grad: bfloat16 [4, 1024, 1024], P('shard', 'ctx'), may hold values from -6 to 6
- segment_ids: int32 [4, 1024], P('shard'), may hold values from 0 to 3, never falling along the last dimension, each value on 1 to 512 neighbouring positions
- w_qkv: bfloat16 [3, 1024, 1024], P(None, 'shard', 'tp'), may hold values from -0.1875 to 0.1875
- bias_qv: float32 [2, 1024], P(None, 'tp'), may hold values from -3 to 3
- w_out: bfloat16 [1024, 1024], P('tp', 'shard'), may hold values from -0.75 to 0.75
- bias_out: float32 [1024], replicated, may hold values from -3 to 3
- norm1_gain: float32 [1024], replicated, may hold values from 0.5 to 1.5
- norm1_shift: float32 [1024], replicated, may hold values from -3 to 3
- w_up: bfloat16 [1024, 4096], P('shard', 'tp'), may hold values from -0.1875 to 0.1875
- bias_up: float32 [4096], P('tp'), may hold values from -3 to 3
- w_down: bfloat16 [4096, 1024], P('tp', 'shard'), may hold values from -0.09375 to 0.09375
- bias_down: float32 [1024], replicated, may hold values from -3 to 3
- norm2_gain: float32 [1024], replicated, may hold values from 0.5 to 1.5
- norm2_shift: float32 [1024], replicated, may hold values from -3 to 3
Outputs:
- output: bfloat16 [4, 1024, 1024], P('shard', 'ctx')
- input_grad: bfloat16 [4, 1024, 1024], P('shard', 'ctx')
- w_qkv_grad: float32 [3, 1024, 1024], P(None, 'shard', 'tp')
- bias_qv_grad: float32 [2, 1024], P(None, 'tp')
- w_out_grad: float32 [1024, 1024], P('tp', 'shard')
- bias_out_grad: float32 [1024], replicated
- norm1_gain_grad: float32 [1024], replicated
- norm1_shift_grad: float32 [1024], replicated
- w_up_grad: float32 [1024, 4096], P('shard', 'tp')
- bias_up_grad: float32 [4096], P('tp')
- w_down_grad: float32 [4096, 1024], P('tp', 'shard')
- bias_down_grad: float32 [1024], replicated
- norm2_gain_grad: float32 [1024], replicated
- norm2_shift_grad: float32 [1024], replicated
Inputs may be any that keep to these rules, and one draw needn't show every extreme that they name: `segment_ids`: within each sequence the ids never fall and start at 0; each document has at most 512 tokens, and some document has exactly that many.
All inputs are finite; a program needn't handle non-finite values.
Results may differ from a plain program's by a relative error of at most 0.022.
The roundings to bfloat16 on the way count: a program that leaves them out, or rounds other values in their place, can miss the bound.
Values may be sent and summed in bfloat16 or wider, within the bound.
A program may use at most 128 MiB of HBM per device.

v0:
```python
import math
import jax
import jax.numpy as jnp
from jax import lax
from jax.sharding import PartitionSpec as P

HEADS = 16
EPSILON = 1e-05


def normalize(resid, gain, shift):
    average = jnp.mean(resid, axis=-1, keepdims=True)
    centred = resid - average
    variance = jnp.mean(centred * centred, axis=-1, keepdims=True)
    inv_std = lax.rsqrt(variance + EPSILON)
    normed = centred * inv_std
    return (normed * gain + shift, normed, inv_std)


def normalize_back(cotan, normed, inv_std, gain):
    scaled = cotan * gain
    return inv_std * (
        scaled
        - jnp.mean(scaled, axis=-1, keepdims=True)
        - normed * jnp.mean(scaled * normed, axis=-1, keepdims=True)
    )


def gelu_value(pre_act):
    return 0.5 * pre_act * (1.0 + jax.scipy.special.erf(pre_act * 0.7071067811865476))


def gelu_slope(pre_act):
    return (
        0.5 * (1.0 + jax.scipy.special.erf(pre_act * 0.7071067811865476))
        + pre_act * jnp.exp(-0.5 * pre_act * pre_act) * 0.3989422804014327
    )


def block_scores(query_block, keys, ids_block, ids_whole, scale):
    scores = (
        jnp.einsum("qhe,khe->hqk", query_block, keys, preferred_element_type=jnp.float32) * scale
    )
    return jnp.where((ids_block[:, None] == ids_whole[None, :])[None], scores, -jnp.inf)


def shards(
    hidden_in,
    out_grad,
    segment_ids,
    w_qkv,
    bias_qv,
    w_out,
    bias_out,
    norm1_gain,
    norm1_shift,
    w_up,
    bias_up,
    w_down,
    bias_down,
    norm2_gain,
    norm2_shift,
):
    seq_count, local_len, width = hidden_in.shape
    ctx_count = lax.axis_size("ctx")
    full_len = local_len * ctx_count
    row_count = seq_count * local_len
    head_dim = width // HEADS
    scale = 1.0 / math.sqrt(head_dim)
    qkv_full, out_full, up_full, down_full = (
        lax.all_gather(w_qkv, "shard", axis=1, tiled=True),
        lax.all_gather(w_out, "shard", axis=1, tiled=True),
        lax.all_gather(w_up, "shard", axis=0, tiled=True),
        lax.all_gather(w_down, "shard", axis=1, tiled=True),
    )
    local_cols = qkv_full.shape[2]
    group_cols = local_cols // ctx_count
    local_heads = group_cols // head_dim
    block_rows = min(512, full_len)
    block_count = full_len // block_rows
    tokens = hidden_in.reshape(row_count, width)
    bias_three = jnp.stack([bias_qv[0], jnp.zeros_like(bias_qv[0]), bias_qv[1]])
    project = (
        jnp.einsum("td,kde->tke", tokens, qkv_full, preferred_element_type=jnp.float32)
        + bias_three[None]
    )
    project = project.astype(jnp.bfloat16).reshape(seq_count, local_len, 3, ctx_count, group_cols)
    heads = lax.all_to_all(project, "ctx", split_axis=3, concat_axis=1, tiled=True)
    heads = heads.reshape(seq_count, full_len, 3, local_heads, head_dim)

    def attend_sequence(packed):
        seq_heads, seq_ids = packed
        keys = seq_heads[:, 1]
        values = seq_heads[:, 2]
        queries = seq_heads[:, 0].reshape(block_count, block_rows, local_heads, head_dim)
        id_blocks = seq_ids.reshape(block_count, block_rows)

        def attend_block(piece):
            query_block, ids_block = piece
            scores = block_scores(query_block, keys, ids_block, seq_ids, scale)
            log_total = jax.nn.logsumexp(scores, axis=-1)
            probs_low = jnp.exp(scores - log_total[..., None]).astype(jnp.bfloat16)
            attended = jnp.einsum(
                "hqk,khe->qhe", probs_low, values, preferred_element_type=jnp.float32
            ).astype(jnp.bfloat16)
            return (attended, log_total)

        attended, log_total = lax.map(attend_block, (queries, id_blocks))
        return (attended.reshape(full_len, local_heads, head_dim), log_total)

    attended_heads, log_totals = lax.map(attend_sequence, (heads, segment_ids))
    attended_tok = lax.all_to_all(
        attended_heads.reshape(seq_count, full_len, 1, group_cols),
        "ctx",
        split_axis=1,
        concat_axis=2,
        tiled=True,
    )
    attended_tok = attended_tok.reshape(row_count, local_cols)
    attn_part = jnp.dot(attended_tok, out_full, preferred_element_type=jnp.float32)
    resid_one = (
        lax.psum(attn_part.astype(jnp.bfloat16), "tp").astype(jnp.float32)
        + bias_out
        + tokens.astype(jnp.float32)
    )
    first, normed_one, inv_one = normalize(resid_one, norm1_gain, norm1_shift)
    first_low = first.astype(jnp.bfloat16)
    pre_act = jnp.dot(first_low, up_full, preferred_element_type=jnp.float32) + bias_up
    activated = gelu_value(pre_act).astype(jnp.bfloat16)
    ffn_part = jnp.dot(activated, down_full, preferred_element_type=jnp.float32)
    resid_two = (
        lax.psum(ffn_part.astype(jnp.bfloat16), "tp").astype(jnp.float32) + bias_down + first
    )
    result, normed_two, inv_two = normalize(resid_two, norm2_gain, norm2_shift)
    grad_float = out_grad.reshape(row_count, width).astype(jnp.float32)
    gain_two_grad = jnp.sum(grad_float * normed_two, axis=0)
    shift_two_grad = jnp.sum(grad_float, axis=0)
    resid_two_grad = normalize_back(grad_float, normed_two, inv_two, norm2_gain)
    resid_two_low = resid_two_grad.astype(jnp.bfloat16)
    bias_down_grad = jnp.sum(resid_two_grad, axis=0)
    act_grad = jnp.dot(resid_two_low, down_full.T, preferred_element_type=jnp.float32)
    pre_grad = act_grad * gelu_slope(pre_act)
    pre_low = pre_grad.astype(jnp.bfloat16)
    bias_up_grad = jnp.sum(pre_grad, axis=0)
    back_part = jnp.dot(pre_low, up_full.T, preferred_element_type=jnp.float32)
    first_grad = resid_two_grad + lax.psum(back_part.astype(jnp.bfloat16), "tp").astype(jnp.float32)
    gain_one_grad = jnp.sum(first_grad * normed_one, axis=0)
    shift_one_grad = jnp.sum(first_grad, axis=0)
    resid_one_grad = normalize_back(first_grad, normed_one, inv_one, norm1_gain)
    resid_one_low = resid_one_grad.astype(jnp.bfloat16)
    bias_out_grad = jnp.sum(resid_one_grad, axis=0)
    attended_grad = jnp.dot(resid_one_low, out_full.T, preferred_element_type=jnp.float32).astype(
        jnp.bfloat16
    )
    grad_heads = lax.all_to_all(
        attended_grad.reshape(seq_count, local_len, ctx_count, group_cols),
        "ctx",
        split_axis=2,
        concat_axis=1,
        tiled=True,
    )
    grad_heads = grad_heads.reshape(seq_count, full_len, local_heads, head_dim)

    def back_sequence(packed):
        seq_heads, seq_ids, seq_attended, seq_grad, seq_log = packed
        keys = seq_heads[:, 1]
        values = seq_heads[:, 2]
        queries = seq_heads[:, 0].reshape(block_count, block_rows, local_heads, head_dim)
        id_blocks = seq_ids.reshape(block_count, block_rows)
        att_blocks = seq_attended.reshape(block_count, block_rows, local_heads, head_dim)
        grad_blocks = seq_grad.reshape(block_count, block_rows, local_heads, head_dim)

        def back_block(carry, piece):
            key_total, value_total = carry
            query_block, ids_block, att_block, grad_block, log_block = piece
            scores = block_scores(query_block, keys, ids_block, seq_ids, scale)
            probs = jnp.exp(scores - log_block[..., None])
            probs_low = probs.astype(jnp.bfloat16)
            prob_grad = jnp.einsum(
                "qhe,khe->hqk", grad_block, values, preferred_element_type=jnp.float32
            )
            offset = jnp.sum(
                grad_block.astype(jnp.float32) * att_block.astype(jnp.float32), axis=-1
            ).T
            score_grad = (probs * (prob_grad - offset[..., None]) * scale).astype(jnp.bfloat16)
            query_grad = jnp.einsum(
                "hqk,khe->qhe", score_grad, keys, preferred_element_type=jnp.float32
            ).astype(jnp.bfloat16)
            key_total = key_total + jnp.einsum(
                "hqk,qhe->khe", score_grad, query_block, preferred_element_type=jnp.float32
            )
            value_total = value_total + jnp.einsum(
                "hqk,qhe->khe", probs_low, grad_block, preferred_element_type=jnp.float32
            )
            return ((key_total, value_total), query_grad)

        empty = jnp.zeros((full_len, local_heads, head_dim), jnp.float32)
        (key_total, value_total), query_grads = lax.scan(
            back_block, (empty, empty), (queries, id_blocks, att_blocks, grad_blocks, seq_log)
        )
        return jnp.stack(
            [
                query_grads.reshape(full_len, local_heads, head_dim),
                key_total.astype(jnp.bfloat16),
                value_total.astype(jnp.bfloat16),
            ],
            axis=1,
        )

    head_grads = lax.map(
        back_sequence, (heads, segment_ids, attended_heads, grad_heads, log_totals)
    )
    proj_grad = lax.all_to_all(
        head_grads.reshape(seq_count, full_len, 3, 1, group_cols),
        "ctx",
        split_axis=1,
        concat_axis=3,
        tiled=True,
    )
    proj_grad = proj_grad.reshape(row_count, 3, local_cols)
    bias_qv_grad = jnp.stack(
        [
            jnp.sum(proj_grad[:, 0].astype(jnp.float32), axis=0),
            jnp.sum(proj_grad[:, 2].astype(jnp.float32), axis=0),
        ]
    )
    input_part = jnp.einsum("tke,kde->td", proj_grad, qkv_full, preferred_element_type=jnp.float32)
    input_grad = (
        resid_one_grad + lax.psum(input_part.astype(jnp.bfloat16), "tp").astype(jnp.float32)
    ).astype(jnp.bfloat16)
    shard_rows = width // lax.axis_size("shard")
    part_qkv = jnp.einsum(
        "td,tke->dke", tokens, proj_grad, preferred_element_type=jnp.float32
    ).reshape(shard_rows * lax.axis_size("shard"), 3 * local_cols)
    part_out = jnp.einsum(
        "td,te->de", resid_one_low, attended_tok, preferred_element_type=jnp.float32
    )
    part_up = jnp.einsum("td,te->de", first_low, pre_low, preferred_element_type=jnp.float32)
    part_down = jnp.einsum(
        "td,te->de", resid_two_low, activated, preferred_element_type=jnp.float32
    )
    owned = lax.psum_scatter(
        jnp.concatenate([part_qkv, part_out, part_up, part_down], axis=1).astype(jnp.bfloat16),
        "shard",
        scatter_dimension=0,
        tiled=True,
    ).astype(jnp.float32)
    owned = lax.psum(owned.astype(jnp.bfloat16), "ctx").astype(jnp.float32)
    owned_rows = owned.shape[0]
    hidden_cols = pre_low.shape[1]
    qkv_grad = owned[:, : 3 * local_cols].reshape(owned_rows, 3, local_cols).transpose(1, 0, 2)
    out_weight_grad = owned[:, 3 * local_cols : 4 * local_cols].T
    up_grad = owned[:, 4 * local_cols : 4 * local_cols + hidden_cols]
    down_grad = owned[:, 4 * local_cols + hidden_cols :].T
    small = lax.psum(
        (
            bias_qv_grad,
            bias_out_grad,
            gain_one_grad,
            shift_one_grad,
            bias_up_grad,
            bias_down_grad,
            gain_two_grad,
            shift_two_grad,
        ),
        ("shard", "ctx"),
    )
    output = result.astype(jnp.bfloat16).reshape(seq_count, local_len, width)
    return (
        output,
        input_grad.reshape(seq_count, local_len, width),
        qkv_grad,
        small[0],
        out_weight_grad,
        small[1],
        small[2],
        small[3],
        up_grad,
        small[4],
        down_grad,
        small[5],
        small[6],
        small[7],
    )


def solution(mesh):
    return jax.shard_map(
        shards,
        mesh=mesh,
        in_specs=(
            P("shard", "ctx", None),
            P("shard", "ctx", None),
            P("shard", None),
            P(None, "shard", "tp"),
            P(None, "tp"),
            P("tp", "shard"),
            P(),
            P(),
            P(),
            P("shard", "tp"),
            P("tp"),
            P("tp", "shard"),
            P(),
            P(),
            P(),
        ),
        out_specs=(
            P("shard", "ctx", None),
            P("shard", "ctx", None),
            P(None, "shard", "tp"),
            P(None, "tp"),
            P("tp", "shard"),
            P(),
            P(),
            P(),
            P("shard", "tp"),
            P("tp"),
            P("tp", "shard"),
            P(),
            P(),
            P(),
        ),
        check_vma=False,
    )
```

profile of v0, /device:TPU:0, one launch (start us, length us, event | category | flops | bytes accessed | tf_op | source)
XLA Modules:
  0.0 789.5 jit_solution(12445965865894515886)
XLA Ops:
  8.8 66.9 %all-gather.5.cloned.1.call-done = bf16[3,1024,512]{2,1,0:T(8,128)(2,1)} async-done(((bf16[3,256,512]{2,1,0:T(8,128)(2,1)}), bf16[3,1024,512]{2,1,0:T(8,128)(2,1)}) %all-gather.5.cloned.1.call-update) | async-done | bytes 3145744 | tf_op jit(solution)/shard_map/all_gather | solution.py:71
  75.8 3.0 add_convert_fusion
  80.0 3.5 all-to-all-start
  85.5 9.6 %all-to-all-done = bf16[1,256,3,4,128]{4,1,2,0,3:T(8,128)(2,1)S(1)} async-done(((bf16[1,256,3,4,128]{4,1,2,0,3:T(8,128)(2,1)}), bf16[1,256,3,4,128]{4,1,2,0,3:T(8,128)(2,1)S(1)}, u32[]{:S(2)}, u32[]{:S(2)}) %all-to-all-start) | async-done | bytes 786464 | tf_op jit(solution)/shard_map/all_to_all | solution.py:88
  96.7 7.9 %while.45 = (s32[]{:T(128)}, bf16[2,512,2,64]{1,3,2,0:T(8,128)(2,1)S(1)}, f32[2,2,512]{2,1,0:T(2,128)S(1)}, s32[2,512]{1,0:T(2,128)S(1)}, s32[1024]{0:T(1024)S(1...) while((s32[]{:T(128)}, ...), condition=%wide.region_3.4_spmd, body=%wide.region_0.3_spmd.sunk | while | flops 280567808 | bytes 15526005 | solution.py:108
  105.9 2.3 reduce.7
  108.2 8.4 %all_to_all.60 = bf16[4,2,16384]{2,1,0:T(2,128)(2,1)S(1)} all-to-all(bf16[4,2,16384]{2,1,0:T(2,128)(2,1)S(1)} %reshape.279), channel_id=1, replica_groups=mesh['shard'=4,'ctx'=4,'tp'=2] {'ctx'}, dimensions={0} | all-to-all | bytes 524288 | tf_op jit(solution)/shard_map/all_to_all | solution.py:112
  117.2 2.6 convolution_convert_fusion.5
  121.1 25.2 %all-reduce.7.cloned.1.call-done = bf16[256,1024]{1,0:T(8,128)(2,1)} async-done(((bf16[256,1024]{1,0:T(8,128)(2,1)}), bf16[256,1024]{1,0:T(8,128)(2,1)}) %all-reduce.7.cloned.1.call-update) | async-done | bytes 524304 | tf_op jit(solution)/shard_map/psum | solution.py:122
  147.6 1.4 multiply_reduce_fusion.3
  149.0 79.5 %all-gather.9.cloned.1.call-done = bf16[1024,2048]{1,0:T(8,128)(2,1)} async-done(((bf16[256,2048]{1,0:T(8,128)(2,1)}), bf16[1024,2048]{1,0:T(8,128)(2,1)}) %all-gather.9.cloned.1.call-update) | async-done | bytes 4194320 | tf_op jit(solution)/shard_map/all_gather | solution.py:73
  228.5 5.6 multiply_convert_fusion.1
  234.1 74.8 %all-gather.11.cloned.1.call-done = bf16[2048,1024]{1,0:T(8,128)(2,1)} async-done(((bf16[2048,256]{1,0:T(8,128)(2,1)}), bf16[2048,1024]{1,0:T(8,128)(2,1)}) %all-gather.11.cloned.1.call-update) | async-done | bytes 4194320 | tf_op jit(solution)/shard_map/all_gather | solution.py:74
  309.0 4.6 convolution_convert_fusion.7
  313.6 26.9 %all-reduce.9.cloned.1.call-done = bf16[256,1024]{1,0:T(8,128)(2,1)} async-done(((bf16[256,1024]{1,0:T(8,128)(2,1)}), bf16[256,1024]{1,0:T(8,128)(2,1)}) %all-reduce.9.cloned.1.call-update) | async-done | bytes 524304 | tf_op jit(solution)/shard_map/psum | solution.py:132
  340.6 1.7 fusion.74
  344.4 2.1 fusion.76
  347.5 2.1 convolution_convert_fusion.6
  349.7 28.8 %all-reduce.11.cloned.1.call-done = bf16[256,1024]{1,0:T(8,128)(2,1)} async-done(((bf16[256,1024]{1,0:T(8,128)(2,1)}), bf16[256,1024]{1,0:T(8,128)(2,1)}) %all-reduce.11.cloned.1.call-update) | async-done | bytes 524304 | tf_op jit(solution)/shard_map/psum | solution.py:146
  378.5 1.9 multiply_reduce_fusion
  380.4 1.5 fusion.73
  384.1 1.8 copy.118
  385.9 4.3 all-to-all-start.2
  390.1 4.6 convolution_convert_fusion.2
  397.4 12.0 %while.46 = (s32[]{:T(128)}, f32[1024,2,64]{0,2,1:T(8,128)S(1)}, f32[1024,2,64]{0,2,1:T(8,128)}, bf16[2,512,2,64]{1,3,2,0:T(8,128)(2,1)S(1)}, bf16[2,512,2,64]{1...) while((s32[]{:T(128)}, f32[1024,2,64]{0,2,1:T(8,128)S(1)}, ...), condition=%wide.region_17.18_spmd.clone, body=%wide.region_15.17_spmd.clone.sunk | while | flops 683998208 | bytes 29526284 | solution.py:198
  398.6 1.4 fusion.140
  400.0 2.0 multiply_convert_fusion.3
  404.6 1.4 fusion.140
  406.0 2.0 multiply_convert_fusion.3
  411.0 1.4 copy.106
  412.4 4.2 all-to-all-start.3
  416.8 4.5 convolution_convert_fusion.1
  423.1 8.1 %all-to-all-done.3 = bf16[1,1024,3,1,128]{4,2,3,0,1:T(4,128)(2,1)} async-done(((bf16[1,1024,3,1,128]{4,2,3,0,1:T(4,128)(2,1)}), bf16[1,1024,3,1,128]{4,2,3,0,1:T(4,128)(2,1)}, u32[]{:S(2)}, u32[]{:S(2)}) %all-to-all-start.3) | async-done | bytes 786464 | tf_op jit(solution)/shard_map/all_to_all | solution.py:213
  432.5 1.5 copy.108
  434.0 1.6 reshape.260
  435.7 2.7 convolution_convert_fusion.3
  438.4 4.6 copy.110
  443.0 10.9 %pad_maximum_fusion = bf16[1024,6144]{1,0:T(8,128)(2,1)} fusion(bf16[1024,2048]{1,0:T(8,128)(2,1)} %convolution_convert_fusion.1, bf16[1024,2048]{1,0:T(8,128)(2,1)} %convolution_convert_fusion.2, bf16[1024,512]{1,0:T(8,128)(2,1)} %copy.111, bf16[1024,1536]{1,0:T(8,128)(2,1)} %copy.110), kind=kLoop, calls=%fused_computation.55 | loop fusion | flops 50331648 | bytes 25165824 | tf_op jit(solution)/shard_map/concatenate | solution.py:243
  454.2 3.7 fusion.53
  458.0 207.0 %reduce-scatter.2.cloned.1.call-done = bf16[256,6144]{1,0:T(8,128)(2,1)} async-done(((bf16[1024,6144]{1,0:T(8,128)(2,1)}), bf16[256,6144]{1,0:T(8,128)(2,1)}) %reduce-scatter.2.cloned.1.call-update) | async-done | bytes 3145744 | tf_op jit(solution)/shard_map/reduce_scatter | solution.py:242
  665.3 62.3 %all-reduce = (f32[2,512]{1,0:T(2,128)}, f32[1024]{0:T(1024)}, f32[1024]{0:T(1024)}, f32[1024]{0:T(1024)}, f32[2048]{0:T(1024)}, /*index=5*/f32[1024]{0:T(1024)}, f32[1024]{0:T(1024)}, f32[1024]{0:T(1024)}) all-reduce(f32[2,512]{1,0:T(2,128)S(1)} %pad_maximum_fusion.3, ...), channel_id=1, replica_groups=mesh['shard'=4,'ctx'=4,'tp'=2] {'shard','ctx'}, use_global_device_ids=true, to_apply=%region_23.24 | all-reduce | flops 9216 | bytes 73728 | tf_op jit(solution)/shard_map/psum | solution.py:255
  727.6 2.0 fusion.61
  729.6 39.1 %all-reduce.15.cloned.1.call-done = bf16[256,6144]{1,0:T(8,128)(2,1)} async-done(((bf16[256,6144]{1,0:T(8,128)(2,1)}), bf16[256,6144]{1,0:T(8,128)(2,1)}) %all-reduce.15.cloned.1.call-update) | async-done | bytes 3145744 | tf_op jit(solution)/shard_map/psum | solution.py:248
  768.7 2.6 convert_element_type.134
  772.2 1.5 slice_bitcast_fusion
  774.4 1.6 copy.113
  776.0 2.9 copy.115
  779.9 2.8 slice.60
  (168 shorter events, 39.4 us)
Async XLA Ops:
  7.2 68.6 %all-gather.5.cloned.1.call-start = ((), (), s32[]{:S(2)}) async-start(), calls=%async_computation.5 | async-start | bytes 3932160 | tf_op jit(solution)/shard_map/all_gather | solution.py:71
  8.8 76.0 %copy-start.14 = (s32[1,1024]{1,0:T(1,128)S(1)}, s32[1,1024]{1,0:T(1,128)}, u32[]{:S(2)}) copy-start(s32[1,1024]{1,0:T(1,128)} %param.21) | copy-start | bytes 12292
  80.0 15.1 %all-to-all-start = ((bf16[1,256,3,4,128]{4,1,2,0,3:T(8,128)(2,1)}), bf16[1,256,3,4,128]{4,1,2,0,3:T(8,128)(2,1)S(1)}, u32[]{:S(2)}, u32[]{:S(2)}) async-start(bf16[1,256,3,4,128]{4,1,2,0,3:T(8,128)(2,1)} %copy.95), calls=%async_computation | async-start | bytes 1572864 | tf_op jit(solution)/shard_map/all_to_all | solution.py:88
  83.5 33.6 %all-gather.7.cloned.1.call-start = ((), (), s32[]{:S(2)}) async-start(), calls=%async_computation.6 | async-start | bytes 1310720 | tf_op jit(solution)/shard_map/all_gather | solution.py:72
  84.3 62.0 %all-reduce.7.cloned.1.call-start = ((), (), s32[]{:S(2)}) async-start(), calls=%async_computation.7 | async-start | bytes 1048576 | tf_op jit(solution)/shard_map/psum | solution.py:122
  104.6 0.8 copy-start.16
  105.9 40.4 %copy-start = (bf16[1,256,1024]{2,1,0:T(8,128)(2,1)S(1)}, bf16[1,256,1024]{2,1,0:T(8,128)(2,1)}, u32[]{:S(2)}) copy-start(bf16[1,256,1024]{2,1,0:T(8,128)(2,1)} %param.19) | copy-start | bytes 1572868
  105.9 40.4 %copy-start.15 = (f32[1024]{0:T(1024)S(1)}, f32[1024]{0:T(1024)}, u32[]{:S(2)}) copy-start(f32[1024]{0:T(1024)} %param.25) | copy-start | bytes 12292
  116.6 111.9 %copy-start.18 = (f32[1024]{0:T(1024)S(1)}, f32[1024]{0:T(1024)}, u32[]{:S(2)}) copy-start(f32[1024]{0:T(1024)} %param.26) | copy-start | bytes 12292
  116.6 111.9 %copy-start.19 = (f32[1024]{0:T(1024)S(1)}, f32[1024]{0:T(1024)}, u32[]{:S(2)}) copy-start(f32[1024]{0:T(1024)} %param.27) | copy-start | bytes 12292
  116.6 111.9 %copy-start.25 = (f32[2048]{0:T(1024)S(1)}, f32[2048]{0:T(1024)}, u32[]{:S(2)}) copy-start(f32[2048]{0:T(1024)} %param.29) | copy-start | bytes 24580
  117.1 117.0 %copy-start.8 = (bf16[1,256,4,1,128]{1,4,2,3,0:T(8,128)(2,1)}, bf16[1,256,4,1,128]{1,4,2,3,0:T(8,128)(2,1)S(1)}, u32[]{:S(2)}) copy-start(bf16[1,256,4,1,128]{1,4,2,3,0:T(8,128)(2,1)S(1)} %copy.100) | copy-start | bytes 786436
  119.7 108.7 %all-gather.9.cloned.1.call-start = ((), (), s32[]{:S(2)}) async-start(), calls=%async_computation.8 | async-start | bytes 5242880 | tf_op jit(solution)/shard_map/all_gather | solution.py:73
  120.3 188.6 %all-gather.11.cloned.1.call-start = ((), (), s32[]{:S(2)}) async-start(), calls=%async_computation.9 | async-start | bytes 5242880 | tf_op jit(solution)/shard_map/all_gather | solution.py:74
  120.9 219.7 %all-reduce.9.cloned.1.call-start = ((), (), s32[]{:S(2)}) async-start(), calls=%async_computation.10 | async-start | bytes 1048576 | tf_op jit(solution)/shard_map/psum | solution.py:132
  234.1 106.5 %copy-start.1 = (bf16[256,1024]{1,0:T(8,128)(2,1)S(1)}, bf16[256,1024]{1,0:T(8,128)(2,1)}, u32[]{:S(2)}) copy-start(bf16[256,1024]{1,0:T(8,128)(2,1)} %all-reduce.7.cloned.1.call-done) | copy-start | bytes 1572868
  234.1 106.5 %copy-start.21 = (f32[1024]{0:T(1024)S(1)}, f32[1024]{0:T(1024)}, u32[]{:S(2)}) copy-start(f32[1024]{0:T(1024)} %param.31) | copy-start | bytes 12292
  309.0 33.6 %copy-start.5 = (bf16[1,256,1024]{2,1,0:T(8,128)(2,1)S(1)}, bf16[1,256,1024]{2,1,0:T(8,128)(2,1)}, u32[]{:S(2)}) copy-start(bf16[1,256,1024]{2,1,0:T(8,128)(2,1)} %param.20) | copy-start | bytes 1572868
  309.0 33.7 %copy-start.20 = (f32[1024]{0:T(1024)S(1)}, f32[1024]{0:T(1024)}, u32[]{:S(2)}) copy-start(f32[1024]{0:T(1024)} %param.32) | copy-start | bytes 12292
  313.6 29.6 %copy-start.22 = (f32[1024]{0:T(1024)S(1)}, f32[1024]{0:T(1024)}, u32[]{:S(2)}) copy-start(f32[1024]{0:T(1024)} %param.33) | copy-start | bytes 12292
  313.6 64.9 %all-reduce.11.cloned.1.call-start = ((), (), s32[]{:S(2)}) async-start(), calls=%async_computation.11 | async-start | bytes 1048576 | tf_op jit(solution)/shard_map/psum | solution.py:146
  340.6 3.8 copy-start.24
  340.6 3.8 copy-start.26
  344.4 3.1 copy-start.23
  346.6 1.0 copy-start.11
  378.5 4.4 copy-start.7
  381.9 1.0 copy-start.2
  385.9 10.1 %all-to-all-start.2 = ((bf16[1,256,4,128]{1,3,0,2:T(8,128)(2,1)}), bf16[1,256,4,128]{1,3,0,2:T(8,128)(2,1)}, u32[]{:S(2)}, u32[]{:S(2)}) async-start(bf16[1,256,4,128]{1,3,0,2:T(8,128)(2,1)} %bitcast.233), calls=%async_computation.2 | async-start | bytes 524288 | tf_op jit(solution)/shard_map/all_to_all | solution.py:155
  397.4 1.2 copy-start.12
  398.6 1.4 copy-start.17
  400.0 2.0 copy-start.13
  403.4 1.2 copy-start.12
  404.6 1.4 copy-start.17
  406.0 2.0 copy-start.13
  412.4 18.7 %all-to-all-start.3 = ((bf16[1,1024,3,1,128]{4,2,3,0,1:T(4,128)(2,1)}), bf16[1,1024,3,1,128]{4,2,3,0,1:T(4,128)(2,1)}, u32[]{:S(2)}, u32[]{:S(2)}) async-start(bf16[1,1024,3,1,128]{4,2,3,0,1:T(4,128)(2,1)} %copy.106), calls=%async_computation.3 | async-start | bytes 2097152 | tf_op jit(solution)/shard_map/all_to_all | solution.py:213
  416.7 4.6 copy-start.3
  416.7 4.6 copy-start.9
  416.7 248.3 %reduce-scatter.2.cloned.1.call-start = ((), (), s32[]{:S(2)}) async-start(), calls=%async_computation.13 | async-start | bytes 15728640 | tf_op jit(solution)/shard_map/reduce_scatter | solution.py:242
  453.9 211.2 %copy-start.6 = (bf16[1,256,1024]{2,1,0:T(8,128)(2,1)S(1)}, bf16[1,256,1024]{2,1,0:T(8,128)(2,1)}, u32[]{:S(2)}) copy-start(bf16[1,256,1024]{2,1,0:T(8,128)(2,1)} %param.20) | copy-start | bytes 1572868
  453.9 273.7 %all-reduce.13.cloned.1.call-start = ((), (), s32[]{:S(2)}) async-start(), calls=%async_computation.12 | async-start | bytes 1048576 | tf_op jit(solution)/shard_map/psum | solution.py:229
  458.0 310.7 %all-reduce.15.cloned.1.call-start = ((), (), s32[]{:S(2)}) async-start(), calls=%async_computation.14 | async-start | bytes 6291456 | tf_op jit(solution)/shard_map/psum | solution.py:248
  771.3 2.4 copy-start.4
  774.4 4.5 copy-start.10
Sparse Core Ops, SparseCore 0:
  9.6 66.1 all-gather.4
  85.9 29.0 all-gather.6
  119.9 26.3 all-reduce.6
  147.7 80.7 all-gather.8
  229.9 79.0 all-gather.10
  313.7 26.8 all-reduce.8
  349.8 28.6 all-reduce.10
  454.0 210.9 reduce-scatter.1
  667.9 29.6 all-reduce.12
  699.8 68.8 all-reduce.14
where the time goes:
time: 791 us; the launch traced here: 790 us
  waiting for transfers between devices  570 us (72%)
  blocking collectives  70.7 us (9%)
  matrix products  52.7 us (7%)
  local copies, waits for them, and re-layouts  34.8 us (4%)
  other arithmetic  33.7 us (4%)
  between operations  14.7 us (2%)
  starting transfers between devices  12.8 us (2%)
    reduce_scatter x1, waiting for transfers between devices, shards(): lax.psum_scatter(jnp.concatenate([part_qkv, part_out, part_up, part_down]...  207 us
    all_gather x1, waiting for transfers between devices, shards(): lax.all_gather(w_up, 'shard', axis=0, tiled=True)  79.5 us
    all_gather x1, waiting for transfers between devices, shards(): lax.all_gather(w_down, 'shard', axis=1, tiled=True)  74.8 us
    all_gather x1, waiting for transfers between devices, shards(): lax.all_gather(w_qkv, 'shard', axis=1, tiled=True)  66.9 us
    psum x1, blocking collectives, shards(): lax.psum((bias_qv_grad, bias_out_grad, gain_one_grad, shift_one_grad, bia...  62.3 us
    psum x1, waiting for transfers between devices, shards(): owned = lax.psum(owned.astype(jnp.bfloat16), 'ctx').astype(jnp.float32)  39.1 us
    psum x1, waiting for transfers between devices, shards(): lax.psum(back_part.astype(jnp.bfloat16), 'tp').astype(jnp.float32)  28.8 us
    psum x1, waiting for transfers between devices, shards(): lax.psum(ffn_part.astype(jnp.bfloat16), 'tp').astype(jnp.float32)  26.9 us
  transfers between devices with their start and end apart: 13, of which 11 were waited for; matrix products, arithmetic and copies ran while one was open for 5% of the time, Pallas kernels for 0%

commit v1 on v0

--- a/solution.py
+++ b/solution.py
@@ -6,6 +6,22 @@
 
 HEADS = 16
 EPSILON = 1e-05
+
+
+def gather_around(x, axis, dim):
+    ways, here, hop = (lax.axis_size(axis), lax.axis_index(axis), x.shape[dim])
+    shape = [n * ways if d == dim else n for d, n in enumerate(x.shape)]
+    full = lax.dynamic_update_slice_in_dim(jnp.zeros(shape, x.dtype), x, here * hop, axis=dim)
+    going_up = going_down = x
+    for far in range(1, ways // 2 + 1):
+        going_up = lax.ppermute(going_up, axis, [(d, (d + 1) % ways) for d in range(ways)])
+        full = lax.dynamic_update_slice_in_dim(full, going_up, (here - far) % ways * hop, axis=dim)
+        if 2 * far < ways:
+            going_down = lax.ppermute(going_down, axis, [(d, (d - 1) % ways) for d in range(ways)])
+            full = lax.dynamic_update_slice_in_dim(
+                full, going_down, (here + far) % ways * hop, axis=dim
+            )
+    return full
 
 
 def normalize(resid, gain, shift):
@@ -70,7 +86,7 @@
     qkv_full, out_full, up_full, down_full = (
         lax.all_gather(w_qkv, "shard", axis=1, tiled=True),
         lax.all_gather(w_out, "shard", axis=1, tiled=True),
-        lax.all_gather(w_up, "shard", axis=0, tiled=True),
+        gather_around(w_up, "shard", 0),
         lax.all_gather(w_down, "shard", axis=1, tiled=True),
     )
     local_cols = qkv_full.shape[2]

time: 791 us -> 748 us (0.946)
  waiting for transfers between devices: 570 us -> 506 us
  local copies, waits for them, and re-layouts: 34.8 us -> 50.9 us
    ppermute x0 -> x3, waiting for transfers between devices: none -> 92 us  [the longest x2 56 us: gather_around(): lax.ppermute(going_up, axis, [(d, (d + 1) % ways) for d in range(ways)])]
    all_gather x1 -> x0, waiting for transfers between devices: 79.5 us -> none  [shards(): lax.all_gather(w_up, 'shard', axis=0, tiled=True)]
    all_gather x1, waiting for transfers between devices: 74.8 us -> 24.6 us  [shards(): lax.all_gather(w_down, 'shard', axis=1, tiled=True)]
    psum x1, waiting for transfers between devices: 25.2 us -> 0.01 us  [shards(): lax.psum(attn_part.astype(jnp.bfloat16), 'tp').astype(jnp.float32)]
    dynamic_update_slice x0 -> x4, local copies, waits for them, and re-layouts: none -> 8.09 us  [the longest x2 4.7 us: gather_around(): lax.dynamic_update_slice_in_dim(full, going_up, (here - far) % ways * hop...]
  transfers between devices with their start and end apart: 13 -> 15, of which waited for: 11 -> 12; matrix products, arithmetic and copies ran while one was open for 5% -> 7% of each run, Pallas kernels for 0% -> 0%
where the time goes in v1:
time: 748 us; the launch traced here: 747 us
  waiting for transfers between devices  506 us (68%)
  blocking collectives  70.7 us (9%)
  matrix products  54.2 us (7%)
  local copies, waits for them, and re-layouts  50.9 us (7%)
  other arithmetic  33.7 us (5%)
  starting transfers between devices  16.5 us (2%)
  between operations  14.4 us (2%)
    reduce_scatter x1, waiting for transfers between devices, shards(): lax.psum_scatter(jnp.concatenate([part_qkv, part_out, part_up, part_down]...  207 us
    all_gather x1, waiting for transfers between devices, shards(): lax.all_gather(w_qkv, 'shard', axis=1, tiled=True)  66.9 us
    psum x1, blocking collectives, shards(): lax.psum((bias_qv_grad, bias_out_grad, gain_one_grad, shift_one_grad, bia...  62.3 us
    ppermute x2, waiting for transfers between devices, gather_around(): lax.ppermute(going_up, axis, [(d, (d + 1) % ways) for d in range(ways)])  56 us
    psum x1, waiting for transfers between devices, shards(): owned = lax.psum(owned.astype(jnp.bfloat16), 'ctx').astype(jnp.float32)  39.2 us
    ppermute x1, waiting for transfers between devices, gather_around(): lax.ppermute(going_down, axis, [(d, (d - 1) % ways) for d in range(ways)])  36 us
    psum x1, waiting for transfers between devices, shards(): lax.psum(back_part.astype(jnp.bfloat16), 'tp').astype(jnp.float32)  28.8 us
    psum x1, waiting for transfers between devices, shards(): lax.psum(ffn_part.astype(jnp.bfloat16), 'tp').astype(jnp.float32)  26.3 us
  transfers between devices with their start and end apart: 15, of which 12 were waited for; matrix products, arithmetic and copies ran while one was open for 7% of the time, Pallas kernels for 0%

profile of v1, /device:TPU:0, one launch (start us, length us, event | category | flops | bytes accessed | tf_op | source)
XLA Modules:
  0.0 746.5 jit_solution(5344457241700051919)
XLA Ops:
  8.8 66.9 %all-gather.4.cloned.1.call-done = bf16[3,1024,512]{2,1,0:T(8,128)(2,1)} async-done(((bf16[3,256,512]{2,1,0:T(8,128)(2,1)}), bf16[3,1024,512]{2,1,0:T(8,128)(2,1)}) %all-gather.4.cloned.1.call-update) | async-done | bytes 3145744 | tf_op jit(solution)/shard_map/all_gather | solution.py:87
  75.8 3.0 add_convert_fusion
  80.0 3.5 all-to-all-start
  85.5 9.6 %all-to-all-done = bf16[1,256,3,4,128]{4,1,2,0,3:T(8,128)(2,1)S(1)} async-done(((bf16[1,256,3,4,128]{4,1,2,0,3:T(8,128)(2,1)}), bf16[1,256,3,4,128]{4,1,2,0,3:T(8,128)(2,1)S(1)}, u32[]{:S(2)}, u32[]{:S(2)}) %all-to-all-start) | async-done | bytes 786464 | tf_op jit(solution)/shard_map/all_to_all | solution.py:104
  96.7 7.9 %while.45 = (s32[]{:T(128)}, bf16[2,512,2,64]{1,3,2,0:T(8,128)(2,1)S(1)}, f32[2,2,512]{2,1,0:T(2,128)S(1)}, s32[2,512]{1,0:T(2,128)S(1)}, s32[1024]{0:T(1024)S(1...) while((s32[]{:T(128)}, ...), condition=%wide.region_3.4_spmd, body=%wide.region_0.3_spmd.sunk | while | flops 280567808 | bytes 15526005 | solution.py:124
  106.6 2.2 reduce.7
  108.9 8.4 %all_to_all.60 = bf16[4,2,16384]{2,1,0:T(2,128)(2,1)S(1)} all-to-all(bf16[4,2,16384]{2,1,0:T(2,128)(2,1)S(1)} %reshape.279), channel_id=1, replica_groups=mesh['shard'=4,'ctx'=4,'tp'=2] {'ctx'}, dimensions={0} | all-to-all | bytes 524288 | tf_op jit(solution)/shard_map/all_to_all | solution.py:128
  117.8 2.6 convolution_convert_fusion.5
  121.0 3.8 collective-permute-start.1
  124.9 24.1 %collective-permute-done = bf16[256,2048]{1,0:T(8,128)(2,1)} collective-permute-done((bf16[256,2048]{1,0:T(8,128)(2,1)S(1)}, bf16[256,2048]{1,0:T(8,128)(2,1)}, u32[]{:S(2)}, u32[]{:S(2)}) %collective-permute-start) | collective-permute-done | bytes 1048608 | tf_op jit(solution)/shard_map/ppermute | solution.py:17
  149.0 2.5 broadcast_in_dim.44
  152.5 2.3 constant_dynamic-update-slice_fusion.2
  154.9 36.0 %collective-permute-done.1 = bf16[256,2048]{1,0:T(8,128)(2,1)} collective-permute-done((bf16[256,2048]{1,0:T(8,128)(2,1)S(1)}, bf16[256,2048]{1,0:T(8,128)(2,1)}, u32[]{:S(2)}, u32[]{:S(2)}) %collective-permute-start.1) | collective-permute-done | bytes 1048608 | tf_op jit(solution)/shard_map/ppermute | solution.py:20
  190.9 2.4 constant_dynamic-update-slice_fusion.1
  193.3 31.8 %collective-permute-done.2 = bf16[256,2048]{1,0:T(8,128)(2,1)} collective-permute-done((bf16[256,2048]{1,0:T(8,128)(2,1)}, bf16[256,2048]{1,0:T(8,128)(2,1)}, u32[]{:S(2)}, u32[]{:S(2)}) %collective-permute-start.2) | collective-permute-done | bytes 1048608 | tf_op jit(solution)/shard_map/ppermute | solution.py:17
  225.1 2.3 constant_dynamic-update-slice_fusion
  230.2 5.3 multiply_convert_fusion.1
  235.5 24.6 %all-gather.8.cloned.1.call-done = bf16[2048,1024]{1,0:T(8,128)(2,1)} async-done(((bf16[2048,256]{1,0:T(8,128)(2,1)}), bf16[2048,1024]{1,0:T(8,128)(2,1)}) %all-gather.8.cloned.1.call-update) | async-done | bytes 4194320 | tf_op jit(solution)/shard_map/all_gather | solution.py:90
  260.1 4.3 convolution_convert_fusion.7
  264.4 26.3 %all-reduce.9.cloned.1.call-done = bf16[256,1024]{1,0:T(8,128)(2,1)} async-done(((bf16[256,1024]{1,0:T(8,128)(2,1)}), bf16[256,1024]{1,0:T(8,128)(2,1)}) %all-reduce.9.cloned.1.call-update) | async-done | bytes 524304 | tf_op jit(solution)/shard_map/psum | solution.py:148
  290.7 1.7 fusion.74
  294.5 2.1 fusion.76
  297.6 4.3 convolution_convert_fusion.6
  301.9 28.8 %all-reduce.11.cloned.1.call-done = bf16[256,1024]{1,0:T(8,128)(2,1)} async-done(((bf16[256,1024]{1,0:T(8,128)(2,1)}), bf16[256,1024]{1,0:T(8,128)(2,1)}) %all-reduce.11.cloned.1.call-update) | async-done | bytes 524304 | tf_op jit(solution)/shard_map/psum | solution.py:162
  330.7 1.9 multiply_reduce_fusion
  336.3 1.8 copy.118
  338.1 4.3 all-to-all-start.2
  342.4 4.6 convolution_convert_fusion.2
  349.6 12.0 %while.46 = (s32[]{:T(128)}, f32[1024,2,64]{0,2,1:T(8,128)S(1)}, f32[1024,2,64]{0,2,1:T(8,128)}, bf16[2,512,2,64]{1,3,2,0:T(8,128)(2,1)S(1)}, bf16[2,512,2,64]{1...) while((s32[]{:T(128)}, f32[1024,2,64]{0,2,1:T(8,128)S(1)}, ...), condition=%wide.region_17.18_spmd.clone, body=%wide.region_15.17_spmd.clone.sunk | while | flops 683998208 | bytes 29526284 | solution.py:214
  352.3 2.0 multiply_convert_fusion.3
  358.3 2.0 multiply_convert_fusion.3
  364.7 4.2 all-to-all-start.3
  369.0 4.5 convolution_convert_fusion.1
  375.4 8.1 %all-to-all-done.3 = bf16[1,1024,3,1,128]{4,2,3,0,1:T(4,128)(2,1)} async-done(((bf16[1,1024,3,1,128]{4,2,3,0,1:T(4,128)(2,1)}), bf16[1,1024,3,1,128]{4,2,3,0,1:T(4,128)(2,1)}, u32[]{:S(2)}, u32[]{:S(2)}) %all-to-all-start.3) | async-done | bytes 786464 | tf_op jit(solution)/shard_map/all_to_all | solution.py:229
  386.3 1.6 reshape.260
  388.0 2.7 convolution_convert_fusion.3
  390.6 4.6 copy.110
  395.3 10.9 %pad_maximum_fusion = bf16[1024,6144]{1,0:T(8,128)(2,1)} fusion(bf16[1024,2048]{1,0:T(8,128)(2,1)} %convolution_convert_fusion.1, bf16[1024,2048]{1,0:T(8,128)(2,1)} %convolution_convert_fusion.2, bf16[1024,512]{1,0:T(8,128)(2,1)} %copy.111, bf16[1024,1536]{1,0:T(8,128)(2,1)} %copy.110), kind=kLoop, calls=%fused_computation.55 | loop fusion | flops 50331648 | bytes 25165824 | tf_op jit(solution)/shard_map/concatenate | solution.py:259
  406.5 3.7 fusion.53
  410.3 207.0 %reduce-scatter.2.cloned.1.call-done = bf16[256,6144]{1,0:T(8,128)(2,1)} async-done(((bf16[1024,6144]{1,0:T(8,128)(2,1)}), bf16[256,6144]{1,0:T(8,128)(2,1)}) %reduce-scatter.2.cloned.1.call-update) | async-done | bytes 3145744 | tf_op jit(solution)/shard_map/reduce_scatter | solution.py:258
  617.6 62.3 %all-reduce = (f32[2,512]{1,0:T(2,128)}, f32[1024]{0:T(1024)}, f32[1024]{0:T(1024)}, f32[1024]{0:T(1024)}, f32[2048]{0:T(1024)}, /*index=5*/f32[1024]{0:T(1024)}, f32[1024]{0:T(1024)}, f32[1024]{0:T(1024)}) all-reduce(f32[2,512]{1,0:T(2,128)S(1)} %pad_maximum_fusion.3, ...), channel_id=1, replica_groups=mesh['shard'=4,'ctx'=4,'tp'=2] {'shard','ctx'}, use_global_device_ids=true, to_apply=%region_23.24 | all-reduce | flops 9216 | bytes 73728 | tf_op jit(solution)/shard_map/psum | solution.py:271
  679.9 2.0 fusion.61
  681.9 39.2 %all-reduce.15.cloned.1.call-done = bf16[256,6144]{1,0:T(8,128)(2,1)} async-done(((bf16[256,6144]{1,0:T(8,128)(2,1)}), bf16[256,6144]{1,0:T(8,128)(2,1)}) %all-reduce.15.cloned.1.call-update) | async-done | bytes 3145744 | tf_op jit(solution)/shard_map/psum | solution.py:264
  721.1 2.6 convert_element_type.134
  727.5 3.0 copy.112
  730.5 3.0 copy.113
  733.5 2.9 copy.115
  736.4 2.0 copy.114
  (176 shorter events, 51.8 us)
Async XLA Ops:
  7.2 68.6 %all-gather.4.cloned.1.call-start = ((), (), s32[]{:S(2)}) async-start(), calls=%async_computation.5 | async-start | bytes 3932160 | tf_op jit(solution)/shard_map/all_gather | solution.py:87
  8.8 76.0 %copy-start.15 = (s32[1,1024]{1,0:T(1,128)S(1)}, s32[1,1024]{1,0:T(1,128)}, u32[]{:S(2)}) copy-start(s32[1,1024]{1,0:T(1,128)} %param.21) | copy-start | bytes 12292
  80.0 15.1 %all-to-all-start = ((bf16[1,256,3,4,128]{4,1,2,0,3:T(8,128)(2,1)}), bf16[1,256,3,4,128]{4,1,2,0,3:T(8,128)(2,1)S(1)}, u32[]{:S(2)}, u32[]{:S(2)}) async-start(bf16[1,256,3,4,128]{4,1,2,0,3:T(8,128)(2,1)} %copy.95), calls=%async_computation | async-start | bytes 1572864 | tf_op jit(solution)/shard_map/all_to_all | solution.py:104
  83.5 34.2 %all-gather.6.cloned.1.call-start = ((), (), s32[]{:S(2)}) async-start(), calls=%async_computation.6 | async-start | bytes 1310720 | tf_op jit(solution)/shard_map/all_gather | solution.py:88
  84.3 143.2 %all-reduce.7.cloned.1.call-start = ((), (), s32[]{:S(2)}) async-start(), calls=%async_computation.7 | async-start | bytes 1048576 | tf_op jit(solution)/shard_map/psum | solution.py:138
  104.6 0.7 copy-start.17
  105.7 15.3 %copy-start.11 = (bf16[256,2048]{1,0:T(8,128)(2,1)S(1)}, bf16[256,2048]{1,0:T(8,128)(2,1)}, u32[]{:S(2)}) copy-start(bf16[256,2048]{1,0:T(8,128)(2,1)} %param.28) | copy-start | bytes 3145732
  117.7 31.3 %copy-start.8 = (bf16[1,256,4,1,128]{1,4,2,3,0:T(8,128)(2,1)}, bf16[1,256,4,1,128]{1,4,2,3,0:T(8,128)(2,1)S(1)}, u32[]{:S(2)}) copy-start(bf16[1,256,4,1,128]{1,4,2,3,0:T(8,128)(2,1)S(1)} %copy.100) | copy-start | bytes 786436
  120.3 139.7 %all-gather.8.cloned.1.call-start = ((), (), s32[]{:S(2)}) async-start(), calls=%async_computation.8 | async-start | bytes 5242880 | tf_op jit(solution)/shard_map/all_gather | solution.py:90
  120.9 169.8 %all-reduce.9.cloned.1.call-start = ((), (), s32[]{:S(2)}) async-start(), calls=%async_computation.9 | async-start | bytes 1048576 | tf_op jit(solution)/shard_map/psum | solution.py:148
  121.0 28.0 %collective-permute-start = (bf16[256,2048]{1,0:T(8,128)(2,1)S(1)}, bf16[256,2048]{1,0:T(8,128)(2,1)}, u32[]{:S(2)}, u32[]{:S(2)}) collective-permute-start(bf16[256,2048]{1,0:T(8,128)(2,1)S(1)} %copy-done.11), channel_id=1, source_target_pairs={{0,8},{8,16},{16,24},{24,0},{1,9},{9,17},{17,25},{25,1},{2,10},{10... | collective-permute-start | bytes 3145736 | tf_op jit(solution)/shard_map/ppermute | solution.py:17
  121.0 69.9 %collective-permute-start.1 = (bf16[256,2048]{1,0:T(8,128)(2,1)S(1)}, bf16[256,2048]{1,0:T(8,128)(2,1)}, u32[]{:S(2)}, u32[]{:S(2)}) collective-permute-start(bf16[256,2048]{1,0:T(8,128)(2,1)S(1)} %copy-done.11), channel_id=1, source_target_pairs={{0,24},{8,0},{16,8},{24,16},{1,25},{9,1},{17,9},{25,17},{2,26},{10... | collective-permute-start | bytes 3145736 | tf_op jit(solution)/shard_map/ppermute | solution.py:20
  149.0 76.1 %collective-permute-start.2 = (bf16[256,2048]{1,0:T(8,128)(2,1)}, bf16[256,2048]{1,0:T(8,128)(2,1)}, u32[]{:S(2)}, u32[]{:S(2)}) collective-permute-start(bf16[256,2048]{1,0:T(8,128)(2,1)} %collective-permute-done), channel_id=1, source_target_pairs={{0,8},{8,16},{16,24},{24,0},{1,9},{9,17},{17,25},{25,1},{2,10},{10... | collective-permute-start | bytes 3145736 | tf_op jit(solution)/shard_map/ppermute | solution.py:17
  151.5 76.0 %copy-start = (bf16[1,256,1024]{2,1,0:T(8,128)(2,1)S(1)}, bf16[1,256,1024]{2,1,0:T(8,128)(2,1)}, u32[]{:S(2)}) copy-start(bf16[1,256,1024]{2,1,0:T(8,128)(2,1)} %param.19) | copy-start | bytes 1572868
  151.5 76.0 %copy-start.16 = (f32[1024]{0:T(1024)S(1)}, f32[1024]{0:T(1024)}, u32[]{:S(2)}) copy-start(f32[1024]{0:T(1024)} %param.25) | copy-start | bytes 12292
  152.5 77.6 %copy-start.19 = (f32[1024]{0:T(1024)S(1)}, f32[1024]{0:T(1024)}, u32[]{:S(2)}) copy-start(f32[1024]{0:T(1024)} %param.26) | copy-start | bytes 12292
  152.5 77.6 %copy-start.20 = (f32[1024]{0:T(1024)S(1)}, f32[1024]{0:T(1024)}, u32[]{:S(2)}) copy-start(f32[1024]{0:T(1024)} %param.27) | copy-start | bytes 12292
  152.5 77.6 %copy-start.25 = (f32[2048]{0:T(1024)S(1)}, f32[2048]{0:T(1024)}, u32[]{:S(2)}) copy-start(f32[2048]{0:T(1024)} %param.29) | copy-start | bytes 24580
  235.5 57.0 %copy-start.10 = (bf16[256,2048]{1,0:T(8,128)(2,1)}, bf16[256,2048]{1,0:T(8,128)(2,1)S(1)}, u32[]{:S(2)}) copy-start(bf16[256,2048]{1,0:T(8,128)(2,1)S(1)} %get-tuple-element.422) | copy-start | bytes 3145732
  235.5 55.2 %copy-start.1 = (bf16[256,1024]{1,0:T(8,128)(2,1)S(1)}, bf16[256,1024]{1,0:T(8,128)(2,1)}, u32[]{:S(2)}) copy-start(bf16[256,1024]{1,0:T(8,128)(2,1)} %all-reduce.7.cloned.1.call-done) | copy-start | bytes 1572868
  235.5 55.2 %copy-start.22 = (f32[1024]{0:T(1024)S(1)}, f32[1024]{0:T(1024)}, u32[]{:S(2)}) copy-start(f32[1024]{0:T(1024)} %param.31) | copy-start | bytes 12292
  260.0 32.7 %copy-start.5 = (bf16[1,256,1024]{2,1,0:T(8,128)(2,1)S(1)}, bf16[1,256,1024]{2,1,0:T(8,128)(2,1)}, u32[]{:S(2)}) copy-start(bf16[1,256,1024]{2,1,0:T(8,128)(2,1)} %param.20) | copy-start | bytes 1572868
  260.1 32.7 %copy-start.21 = (f32[1024]{0:T(1024)S(1)}, f32[1024]{0:T(1024)}, u32[]{:S(2)}) copy-start(f32[1024]{0:T(1024)} %param.32) | copy-start | bytes 12292
  264.3 28.9 %copy-start.23 = (f32[1024]{0:T(1024)S(1)}, f32[1024]{0:T(1024)}, u32[]{:S(2)}) copy-start(f32[1024]{0:T(1024)} %param.33) | copy-start | bytes 12292
  264.4 66.4 %all-reduce.11.cloned.1.call-start = ((), (), s32[]{:S(2)}) async-start(), calls=%async_computation.10 | async-start | bytes 1048576 | tf_op jit(solution)/shard_map/psum | solution.py:162
  290.7 3.8 copy-start.24
  290.7 3.8 copy-start.26
  296.6 1.0 copy-start.12
  330.7 4.4 copy-start.7
  334.2 1.0 copy-start.2
  338.1 10.1 %all-to-all-start.2 = ((bf16[1,256,4,128]{1,3,0,2:T(8,128)(2,1)}), bf16[1,256,4,128]{1,3,0,2:T(8,128)(2,1)}, u32[]{:S(2)}, u32[]{:S(2)}) async-start(bf16[1,256,4,128]{1,3,0,2:T(8,128)(2,1)} %bitcast.233), calls=%async_computation.2 | async-start | bytes 524288 | tf_op jit(solution)/shard_map/all_to_all | solution.py:171
  349.7 1.2 copy-start.13
  350.9 1.4 copy-start.18
  352.3 2.0 copy-start.14
  355.7 1.2 copy-start.13
  356.9 1.4 copy-start.18
  358.3 2.0 copy-start.14
  364.7 18.7 %all-to-all-start.3 = ((bf16[1,1024,3,1,128]{4,2,3,0,1:T(4,128)(2,1)}), bf16[1,1024,3,1,128]{4,2,3,0,1:T(4,128)(2,1)}, u32[]{:S(2)}, u32[]{:S(2)}) async-start(bf16[1,1024,3,1,128]{4,2,3,0,1:T(4,128)(2,1)} %copy.106), calls=%async_computation.3 | async-start | bytes 2097152 | tf_op jit(solution)/shard_map/all_to_all | solution.py:229
  369.0 4.6 copy-start.3
  369.0 4.6 copy-start.9
  369.0 248.3 %reduce-scatter.2.cloned.1.call-start = ((), (), s32[]{:S(2)}) async-start(), calls=%async_computation.12 | async-start | bytes 15728640 | tf_op jit(solution)/shard_map/reduce_scatter | solution.py:258
  406.2 211.2 %copy-start.6 = (bf16[1,256,1024]{2,1,0:T(8,128)(2,1)S(1)}, bf16[1,256,1024]{2,1,0:T(8,128)(2,1)}, u32[]{:S(2)}) copy-start(bf16[1,256,1024]{2,1,0:T(8,128)(2,1)} %param.20) | copy-start | bytes 1572868
  406.2 273.7 %all-reduce.13.cloned.1.call-start = ((), (), s32[]{:S(2)}) async-start(), calls=%async_computation.11 | async-start | bytes 1048576 | tf_op jit(solution)/shard_map/psum | solution.py:245
  410.2 310.9 %all-reduce.15.cloned.1.call-start = ((), (), s32[]{:S(2)}) async-start(), calls=%async_computation.13 | async-start | bytes 6291456 | tf_op jit(solution)/shard_map/psum | solution.py:264
  723.7 2.4 copy-start.4
Sparse Core Ops, SparseCore 0:
  9.6 66.1 all-gather.3
  85.9 29.0 all-gather.5
  120.5 26.3 all-reduce.6
  148.3 111.7 all-gather.7
  264.5 26.1 all-reduce.8
  302.0 28.6 all-reduce.10
  406.3 210.9 reduce-scatter.1
  620.2 29.6 all-reduce.12
  652.3 68.7 all-reduce.14
